TPU v7x, 512 devices: a whole 4x4x16 slice. The times are simulated.
512 devices in a mesh: rows: 64 (over y, z), depth: 8 (over x, core).
Axes of the slice: x: 4, y: 4, z: 16, core: 2. Of those that a mesh axis runs over, the one named last changes fastest.
Arguments:
- grid_values: float32 [4, 256, 512, 512], P(None, 'depth', 'rows'), may hold values from -4 to 550, as said below
- image_grad: float32 [3, 512, 512], P(None, 'rows', 'depth'), may hold values from -384 to 384
Outputs:
- grid_grad: float32 [4, 256, 512, 512], P(None, 'depth', 'rows')
Inputs may be any that keep to these rules, and one draw needn't show every extreme that they name: `grid_values`: channel 0 holds nonnegative densities; channels 1 to 3 hold colors within -4 to 4.
All inputs are finite; a program needn't handle non-finite values.
Results may differ from a plain program's by a relative error of at most 0.000029.
Values sent between devices are 32-bit elements; how exact they have to be, the bound alone decides.
A program may use at most 64 MiB of HBM per device.

v0:
```python
import jax
import jax.numpy as jnp
from jax import lax
from jax.sharding import PartitionSpec as P

SMOOTH = 0.01
TV_WEIGHT = 0.05


def prefix(value, axis, combine, identity, reverse):
    count, place = (lax.axis_size(axis), lax.axis_index(axis))
    everything = lax.all_gather(value, axis)
    start = jnp.broadcast_to(jnp.asarray(identity, value.dtype), value.shape)

    def hop(k, before):
        at = count - 1 - k if reverse else k
        reached = at > place if reverse else at < place
        new = combine(before, everything[at])
        return jnp.where(reached, new, before)

    return lax.fori_loop(0, count, hop, start)


def extended(value, sides, width):
    for axis, dim in sides:
        count, length = (lax.axis_size(axis), value.shape[dim])
        up = [(i, (i + 1) % count) for i in range(count - 1)]
        down = [(j, i) for i, j in up]
        last = lax.slice_in_dim(value, length - width, length, axis=dim)
        leading = lax.slice_in_dim(value, 0, width, axis=dim)
        before = lax.ppermute(last, axis, up)
        after = lax.ppermute(leading, axis, down)
        value = jnp.concatenate([before, value, after], axis=dim)
    return value


def slope_of(difference):
    return difference / jnp.sqrt(difference * difference + SMOOTH)


def edge_terms(slopes, axis, position_dev, count_dev):
    edges = slopes.shape[axis]
    position = jnp.arange(edges)
    valid = ((position > 0) | (position_dev > 0)) & (
        (position < edges - 1) | (position_dev < count_dev - 1)
    )
    shape = [1, 1, 1, 1]
    shape[axis] = edges
    slopes = slopes * valid.astype(jnp.float32).reshape(shape)
    lower_side = lax.slice_in_dim(slopes, 0, edges - 1, axis=axis)
    upper_side = lax.slice_in_dim(slopes, 1, edges, axis=axis)
    return lower_side - upper_side


def add_terms(earlier, later_part):
    return earlier + later_part


def shards(grid_values, image_grad):
    depth_count = lax.axis_size("depth")
    depth_place = lax.axis_index("depth")
    rows_count = lax.axis_size("rows")
    rows_place = lax.axis_index("rows")
    total_depth = grid_values.shape[1] * depth_count
    density_field = grid_values[0]
    colors = grid_values[1:]
    full_grad = lax.all_gather(image_grad, "depth", axis=2, tiled=True)
    shaded = jnp.sum(full_grad[:, None] * colors, axis=0)
    optical = density_field / total_depth
    inclusive = jnp.cumsum(optical, axis=0)
    before = inclusive - optical
    slab_optical = inclusive[-1]
    survive = jnp.exp(-optical)
    local_transmit = jnp.exp(-before)
    local_weight = local_transmit * (1.0 - survive)
    emitted = local_weight * shaded
    later_local = jnp.cumsum(emitted[::-1], axis=0)[::-1] - emitted
    slab_light = jnp.sum(emitted, axis=0)
    passed = prefix(slab_optical, "depth", add_terms, jnp.zeros_like(slab_optical), False)
    entering = jnp.exp(-passed)
    beyond_light = prefix(
        entering * slab_light, "depth", add_terms, jnp.zeros_like(slab_light), True
    )
    transmit = entering * local_transmit
    weight = entering * local_weight
    later = entering * later_local + beyond_light
    grad_density = (transmit * survive * shaded - later) / total_depth
    grad_colors = full_grad[:, None] * weight[None]
    render_grad = jnp.concatenate([grad_density[None], grad_colors], axis=0)
    padded = extended(grid_values, (("rows", 2), ("depth", 1)), 1)
    along_depth = padded[:, :, 1:-1]
    depth_slopes = slope_of(along_depth[:, 1:] - along_depth[:, :-1])
    along_rows = padded[:, 1:-1]
    row_slopes = slope_of(along_rows[:, :, 1:] - along_rows[:, :, :-1])
    column_inner = slope_of(grid_values[:, :, :, 1:] - grid_values[:, :, :, :-1])
    column_zeros = jnp.zeros(column_inner.shape[:3] + (1,), jnp.float32)
    column_slopes = jnp.concatenate([column_zeros, column_inner, column_zeros], axis=3)
    tv_grad = edge_terms(depth_slopes, 1, depth_place, depth_count)
    tv_grad = tv_grad + edge_terms(row_slopes, 2, rows_place, rows_count)
    tv_grad = tv_grad + edge_terms(column_slopes, 3, 0, 1)
    return render_grad + TV_WEIGHT * tv_grad


def solution(mesh):
    placed = (P(None, "depth", "rows", None), P(None, "rows", "depth"))
    return jax.shard_map(
        shards,
        mesh=mesh,
        in_specs=placed,
        out_specs=P(None, "depth", "rows", None),
        check_vma=False,
    )
```

profile of v0, /device:TPU:26, one launch (start us, length us, event | category | flops | bytes accessed | tf_op | source)
XLA Modules:
  0.0 85.6 jit_solution(739580152901090811)
XLA Ops:
  0.0 2.9 %fusion.21 = (f32[4,32,1,512]{3,2,1,0:T(1,128)S(1)}, f32[4,32,1,512]{3,2,1,0:T(1,128)S(1)}) fusion(f32[4,32,8,512]{3,2,1,0:T(8,128)} %param.6), kind=kLoop, calls=%fused_computation.53 | loop fusion | bytes 1048576 | tf_op jit(solution)/shard_map/slice | solution.py:30
  2.9 0.7 copy.11
  3.6 3.8 %collective-permute-start = (f32[4,32,1,512]{3,1,2,0:T(8,128)}, f32[4,32,1,512]{3,1,2,0:T(8,128)}, u32[]{:S(2)}, u32[]{:S(2)}) collective-permute-start(f32[4,32,1,512]{3,1,2,0:T(8,128)} %copy.11), channel_id=1, source_target_pairs={{0,8},{8,16},{16,24},{24,32},{32,40},{40,48},{48,56},{56,64},{64,7... | collective-permute-start | bytes 786440 | tf_op jit(solution)/shard_map/ppermute | solution.py:31
  7.4 0.7 copy.12
  8.1 9.7 %collective-permute-start.1 = (f32[4,32,1,512]{3,1,2,0:T(8,128)}, f32[4,32,1,512]{3,1,2,0:T(8,128)}, u32[]{:S(2)}, u32[]{:S(2)}) collective-permute-start(f32[4,32,1,512]{3,1,2,0:T(8,128)} %copy.12), channel_id=1, source_target_pairs={{8,0},{16,8},{24,16},{32,24},{40,32},{48,40},{56,48},{64,56},{72,6... | collective-permute-start | bytes 786440 | tf_op jit(solution)/shard_map/ppermute | solution.py:32
  17.9 0.2 fusion.10
  18.0 0.0 copy-start.4
  18.1 1.9 %rsqrt_multiply_fusion = f32[4,32,8,511]{3,2,1,0:T(8,128)} fusion(f32[4,32,8,512]{3,2,1,0:T(8,128)S(1)} %copy-done), kind=kLoop, calls=%fused_computation.20 | loop fusion | flops 2093056 | bytes 6279168 | tf_op jit(solution)/shard_map/div | solution.py:38
  20.0 0.1 copy.3
  20.1 12.8 %all_gather.12 = f32[8,8,512]{2,1,0:T(8,128)S(1)} all-gather(f32[1,8,512]{2,1,0:T(8,128)S(1)} %slice.77), channel_id=1, replica_groups=mesh['rows'=64,'depth'=8] {'depth'}, dimensions={0}, use_global_device_ids=true | all-gather | bytes 147456 | tf_op jit(solution)/shard_map/all_gather | solution.py:12
  32.9 0.3 while.30
  33.2 0.2 fusion.9
  33.4 14.9 %all_gather.13 = f32[3,8,512]{1,0,2:T(4,128)} all-gather(f32[3,8,64]{1,0,2:T(4,128)S(1)} %copy.3), channel_id=1, replica_groups=mesh['rows'=64,'depth'=8] {'depth'}, dimensions={2}, use_global_device_ids=true | all-gather | bytes 55296 | tf_op jit(solution)/shard_map/all_gather | solution.py:67
  48.2 1.4 %copy.4 = f32[3,8,512]{2,1,0:T(8,128)S(1)} copy(f32[3,8,512]{1,0,2:T(4,128)} %all_gather.13) | data formatting | bytes 98304 | tf_op jit(solution)/shard_map/all_gather | solution.py:67
  49.7 1.5 %multiply_reduce_fusion = (f32[32,8,512]{2,1,0:T(8,128)S(1)}, f32[3,32,8,512]{3,2,1,0:T(8,128)}) fusion(f32[4,32,8,512]{3,2,1,0:T(8,128)S(1)} %copy-done, f32[3,8,512]{2,1,0:T(8,128)S(1)} %copy.4, f32[32,8,512]{2,1,0:T(8,128)S(1)} %fusion.9), kind=kLoop, calls=%fused_computation.21 | loop fusion | flops 1048576 | bytes 4243456 | tf_op jit(solution)/shard_map/reduce_sum | solution.py:68
  51.2 0.8 copy-done.3
  52.0 0.2 fusion.20
  52.2 12.7 %all-gather = f32[64,512]{1,0:T(8,128)S(1)} all-gather(f32[8,512]{1,0:T(8,128)S(1)} %fusion.19), channel_id=2, replica_groups=mesh['rows'=64,'depth'=8] {'depth'}, dimensions={0}, use_global_device_ids=true | all-gather | bytes 147456 | tf_op jit(solution)/shard_map/all_gather | solution.py:12
  65.0 0.3 while.31
  65.2 0.8 rev.6
  66.1 1.2 %fusion.22 = f32[32,8,512]{2,1,0:T(8,128)S(1)} fusion(f32[32,8,512]{2,1,0:T(8,128)} %rev.6), kind=kOutput, calls=%fused_computation.54 | output fusion | flops 4063232 | bytes 1048576 | tf_op jit(solution)/shard_map/jit(cumsum)/reduce_window_sum | solution.py:77
  67.3 1.4 %multiply_bitcast_fusion = f32[1,32,8,512]{3,2,1,0:T(8,128)S(1)} fusion(f32[32,8,512]{2,1,0:T(8,128)S(1)} %get-tuple-element.243, f32[32,8,512]{2,1,0:T(8,128)S(1)} %fusion.22, f32[32,8,512]{2,1,0:T(8,128)} %copy-done.3, f32[4,32,8,512]{3,2,1,0:T(8,128)S(1)} %copy-done, f32[8,512]{1,0:T(8,128)S(1)} %get-tuple-element.195, ...), kind=kLoop, calls=%fused_computation.36 | loop fusion | flops 1572864 | bytes 3178496 | tf_op jit(solution)/shard_map/broadcast_in_dim | solution.py:89
  68.8 0.8 maximum_multiply_fusion
  69.6 1.2 %copy.7 = f32[4,32,1,512]{3,2,1,0:T(1,128)S(1)} copy(f32[4,32,1,512]{3,1,2,0:T(8,128)} %collective-permute-done) | data formatting | bytes 524288 | tf_op jit(solution)/shard_map/ppermute | solution.py:31
  70.8 1.2 %copy.8 = f32[4,32,1,512]{3,2,1,0:T(1,128)S(1)} copy(f32[4,32,1,512]{3,1,2,0:T(8,128)} %collective-permute-done.1) | data formatting | bytes 524288 | tf_op jit(solution)/shard_map/ppermute | solution.py:32
  72.0 0.1 pad_maximum_fusion.8
  72.1 2.7 %collective-permute-start.2 = (f32[4,1,10,512]{3,2,1,0:T(8,128)S(1)}, f32[4,1,10,512]{3,2,1,0:T(8,128)S(1)}, u32[]{:S(2)}, u32[]{:S(2)}) collective-permute-start(f32[4,1,10,512]{3,2,1,0:T(8,128)S(1)} %get-tuple-element.244), channel_id=1, source_target_pairs={{1,0},{2,1},{3,2},{4,3},{5,4},{6,5},{7,6},{9,8},{10,9},{11,10},{12... | collective-permute-start | bytes 245768 | tf_op jit(solution)/shard_map/ppermute | solution.py:32
  74.8 1.9 %collective-permute-start.3 = (f32[4,1,10,512]{3,2,1,0:T(8,128)S(1)}, f32[4,1,10,512]{3,2,1,0:T(8,128)S(1)}, u32[]{:S(2)}, u32[]{:S(2)}) collective-permute-start(f32[4,1,10,512]{3,2,1,0:T(8,128)S(1)} %get-tuple-element.245), channel_id=1, source_target_pairs={{0,1},{1,2},{2,3},{3,4},{4,5},{5,6},{6,7},{8,9},{9,10},{10,11},{11... | collective-permute-start | bytes 245768 | tf_op jit(solution)/shard_map/ppermute | solution.py:31
  76.7 1.4 %multiply_multiply_fusion = f32[4,32,9,512]{3,2,1,0:T(8,128)S(1)} fusion(f32[4,32,8,512]{3,2,1,0:T(8,128)S(1)} %copy-done, f32[4,32,1,512]{3,2,1,0:T(1,128)S(1)} %copy.7, f32[4,32,1,512]{3,2,1,0:T(1,128)S(1)} %copy.8, f32[9]{0:T(128)S(1)} %and_convert_fusion), kind=kLoop, calls=%fused_computation.3 | loop fusion | flops 4128768 | bytes 4980772 | tf_op jit(solution)/shard_map/mul | solution.py:49
  78.1 3.0 %collective-permute-done.3 = f32[4,1,10,512]{3,2,1,0:T(8,128)S(1)} collective-permute-done((f32[4,1,10,512]{3,2,1,0:T(8,128)S(1)}, f32[4,1,10,512]{3,2,1,0:T(8,128)S(1)}, u32[]{:S(2)}, u32[]{:S(2)}) %collective-permute-start.3) | collective-permute-done | bytes 81952 | tf_op jit(solution)/shard_map/ppermute | solution.py:31
  81.1 1.9 %multiply_multiply_fusion.1 = f32[4,33,8,512]{3,2,1,0:T(8,128)S(1)} fusion(f32[4,32,1,512]{3,2,1,0:T(1,128)S(1)} %copy.8, f32[4,32,8,512]{3,2,1,0:T(8,128)S(1)} %copy-done, f32[4,32,1,512]{3,2,1,0:T(1,128)S(1)} %copy.7, f32[4,1,10,512]{3,2,1,0:T(8,128)S(1)} %collective-permute-done.3, f32[4,1,10,512]{3,2,1,0:T(8,128)S(1)} %collective-permute-done.2, ...), kind=kLoop, calls=%fused_computation.12 | loop fusion | flops 5947392 | bytes 4948100 | tf_op jit(solution)/shard_map/mul | solution.py:49
  83.0 2.6 %fusion.3 = f32[4,32,8,512]{3,2,1,0:T(8,128)} fusion(f32[4,32,8,513]{3,2,1,0:T(8,128)S(1)} %maximum_multiply_fusion, f32[4,32,9,512]{3,2,1,0:T(8,128)S(1)} %multiply_multiply_fusion, f32[4,33,8,512]{3,2,1,0:T(8,128)S(1)} %multiply_multiply_fusion.1, f32[3,32,8,512]{3,2,1,0:T(8,128)S(1)} %copy-done.2, f32[1,32,8,512]{3,2,1,0:T(8,128)S(1)} %multiply_bitcast_fusion), kind=kLoop, calls=%fused_computation.16 | loop fusion | flops 4194304 | bytes 16777216 | tf_op jit(solution)/shard_map/add | solution.py:101
  (36 shorter events, 0.3 us)
Async XLA Ops:
  0.0 17.9 %copy-start = (f32[4,32,8,512]{3,2,1,0:T(8,128)S(1)}, f32[4,32,8,512]{3,2,1,0:T(8,128)}, u32[]{:S(2)}) copy-start(f32[4,32,8,512]{3,2,1,0:T(8,128)} %param.6) | copy-start | bytes 6291460
  3.6 65.9 %collective-permute-start = (f32[4,32,1,512]{3,1,2,0:T(8,128)}, f32[4,32,1,512]{3,1,2,0:T(8,128)}, u32[]{:S(2)}, u32[]{:S(2)}) collective-permute-start(f32[4,32,1,512]{3,1,2,0:T(8,128)} %copy.11), channel_id=1, source_target_pairs={{0,8},{8,16},{16,24},{24,32},{32,40},{40,48},{48,56},{56,64},{64,7... | collective-permute-start | bytes 786440 | tf_op jit(solution)/shard_map/ppermute | solution.py:31
  8.1 62.6 %collective-permute-start.1 = (f32[4,32,1,512]{3,1,2,0:T(8,128)}, f32[4,32,1,512]{3,1,2,0:T(8,128)}, u32[]{:S(2)}, u32[]{:S(2)}) collective-permute-start(f32[4,32,1,512]{3,1,2,0:T(8,128)} %copy.12), channel_id=1, source_target_pairs={{8,0},{16,8},{24,16},{32,24},{40,32},{48,40},{56,48},{64,56},{72,6... | collective-permute-start | bytes 786440 | tf_op jit(solution)/shard_map/ppermute | solution.py:32
  18.0 2.0 %copy-start.4 = (f32[3,8,64]{2,1,0:T(8,128)S(1)}, f32[3,8,64]{2,1,0:T(8,128)}, u32[]{:S(2)}) copy-start(f32[3,8,64]{2,1,0:T(8,128)} %param.7) | copy-start | bytes 18436
  51.2 0.8 copy-start.3
  66.1 2.7 %copy-start.1 = (f32[4,32,8,511]{3,2,1,0:T(8,128)S(1)}, f32[4,32,8,511]{3,2,1,0:T(8,128)}, u32[]{:S(2)}) copy-start(f32[4,32,8,511]{3,2,1,0:T(8,128)} %rsqrt_multiply_fusion) | copy-start | bytes 6279172
  72.1 6.1 %collective-permute-start.2 = (f32[4,1,10,512]{3,2,1,0:T(8,128)S(1)}, f32[4,1,10,512]{3,2,1,0:T(8,128)S(1)}, u32[]{:S(2)}, u32[]{:S(2)}) collective-permute-start(f32[4,1,10,512]{3,2,1,0:T(8,128)S(1)} %get-tuple-element.244), channel_id=1, source_target_pairs={{1,0},{2,1},{3,2},{4,3},{5,4},{6,5},{7,6},{9,8},{10,9},{11,10},{12... | collective-permute-start | bytes 245768 | tf_op jit(solution)/shard_map/ppermute | solution.py:32
  74.8 6.3 %collective-permute-start.3 = (f32[4,1,10,512]{3,2,1,0:T(8,128)S(1)}, f32[4,1,10,512]{3,2,1,0:T(8,128)S(1)}, u32[]{:S(2)}, u32[]{:S(2)}) collective-permute-start(f32[4,1,10,512]{3,2,1,0:T(8,128)S(1)} %get-tuple-element.245), channel_id=1, source_target_pairs={{0,1},{1,2},{2,3},{3,4},{4,5},{5,6},{6,7},{8,9},{9,10},{10,11},{11... | collective-permute-start | bytes 245768 | tf_op jit(solution)/shard_map/ppermute | solution.py:31
  78.1 4.9 %copy-start.2 = (f32[3,32,8,512]{3,2,1,0:T(8,128)S(1)}, f32[3,32,8,512]{3,2,1,0:T(8,128)}, u32[]{:S(2)}) copy-start(f32[3,32,8,512]{3,2,1,0:T(8,128)} %get-tuple-element.249) | copy-start | bytes 4718596
where the time goes:
time: 86 us; the launch traced here: 85.6 us
  blocking collectives  40.4 us (47%)
  starting transfers between devices  18.1 us (21%)
  other arithmetic  13.5 us (16%)
  local copies, waits for them, and re-layouts  9.99 us (12%)
  waiting for transfers between devices  2.97 us (3%)
    all_gather x2, blocking collectives, prefix(): everything = lax.all_gather(value, axis)  25.5 us
    all_gather x1, blocking collectives, shards(): full_grad = lax.all_gather(image_grad, 'depth', axis=2, tiled=True)  14.9 us
    ppermute x2, starting transfers between devices, extended(): after = lax.ppermute(leading, axis, down)  12.4 us
    ppermute x2, starting transfers between devices, extended(): before = lax.ppermute(last, axis, up)  5.74 us
    mul x3, other arithmetic, edge_terms(): slopes = slopes * valid.astype(jnp.float32).reshape(shape)  4.05 us
    ppermute x2, waiting for transfers between devices, extended(): before = lax.ppermute(last, axis, up)  2.96 us
    slice x1, local copies, waits for them, and re-layouts, extended(): leading = lax.slice_in_dim(value, 0, width, axis=dim)  2.89 us
    add x1, other arithmetic, shards(): return render_grad + TV_WEIGHT * tv_grad  2.61 us
  transfers between devices with their start and end apart: 4, of which 1 were waited for; matrix products, arithmetic and copies ran while one was open for 16% of the time, Pallas kernels for 0%

commit v1 on v0

--- a/solution.py
+++ b/solution.py
@@ -64,7 +64,9 @@
     total_depth = grid_values.shape[1] * depth_count
     density_field = grid_values[0]
     colors = grid_values[1:]
-    full_grad = lax.all_gather(image_grad, "depth", axis=2, tiled=True)
+    full_grad = jnp.concatenate(
+        lax.all_to_all(jnp.stack([image_grad] * lax.axis_size("depth")), "depth", 0, 0), axis=2
+    )
     shaded = jnp.sum(full_grad[:, None] * colors, axis=0)
     optical = density_field / total_depth
     inclusive = jnp.cumsum(optical, axis=0)

time: 86 us -> 80.1 us (0.931)
  blocking collectives: 40.4 us -> 25.5 us
  starting transfers between devices: 18.1 us -> 23 us
  other arithmetic: 13.5 us -> 15.6 us
  local copies, waits for them, and re-layouts: 9.99 us -> 11.9 us
    all_gather x1 -> x0, blocking collectives: 14.9 us -> none  [shards(): full_grad = lax.all_gather(image_grad, 'depth', axis=2, tiled=True)]
    all_to_all x0 -> x1, starting transfers between devices: none -> 4.83 us  [shards(): lax.all_to_all(jnp.stack([image_grad] * lax.axis_size('depth')), 'depth',...]
    unnamed x13 -> x14, local copies, waits for them, and re-layouts: 2.33 us -> 4.37 us
    mul x3, other arithmetic: 4.05 us -> 5.54 us  [edge_terms(): slopes = slopes * valid.astype(jnp.float32).reshape(shape)]
    all_gather x1 -> x0, local copies, waits for them, and re-layouts: 1.45 us -> none  [shards(): full_grad = lax.all_gather(image_grad, 'depth', axis=2, tiled=True)]
    another operation x0 -> x1, local copies, waits for them, and re-layouts: none -> 0.86 us  [shards(): jnp.stack([image_grad] * lax.axis_size('depth'))]
  transfers between devices with their start and end apart: 4 -> 5, of which waited for: 1 -> 1; matrix products, arithmetic and copies ran while one was open for 16% -> 23% of each run, Pallas kernels for 0% -> 0%
where the time goes in v1:
time: 80.1 us; the launch traced here: 79.6 us
  blocking collectives  25.5 us (32%)
  starting transfers between devices  23 us (29%)
  other arithmetic  15.6 us (19%)
  local copies, waits for them, and re-layouts  11.9 us (15%)
  waiting for transfers between devices  2.96 us (4%)
    all_gather x2, blocking collectives, prefix(): everything = lax.all_gather(value, axis)  25.5 us
    ppermute x2, starting transfers between devices, extended(): after = lax.ppermute(leading, axis, down)  12.4 us
    ppermute x2, starting transfers between devices, extended(): before = lax.ppermute(last, axis, up)  5.74 us
    mul x3, other arithmetic, edge_terms(): slopes = slopes * valid.astype(jnp.float32).reshape(shape)  5.54 us
    all_to_all x1, starting transfers between devices, shards(): lax.all_to_all(jnp.stack([image_grad] * lax.axis_size('depth')), 'depth',...  4.83 us
    unnamed x14, local copies, waits for them, and re-layouts  4.37 us
    ppermute x2, waiting for transfers between devices, extended(): before = lax.ppermute(last, axis, up)  2.95 us
    slice x1, local copies, waits for them, and re-layouts, extended(): leading = lax.slice_in_dim(value, 0, width, axis=dim)  2.77 us
  transfers between devices with their start and end apart: 5, of which 1 were waited for; matrix products, arithmetic and copies ran while one was open for 23% of the time, Pallas kernels for 0%

profile of v1, /device:TPU:26, one launch (start us, length us, event | category | flops | bytes accessed | tf_op | source)
XLA Modules:
  0.0 79.6 jit_solution(6938027791226702252)
XLA Ops:
  0.0 0.9 %stack.2 = f32[8,3,8,64]{3,2,1,0:T(8,128)S(1)} broadcast(f32[3,8,64]{2,1,0:T(8,128)} %param.7), dimensions={1,2,3} | broadcast | bytes 55296 | tf_op jit(solution)/shard_map/stack | solution.py:68
  0.9 0.7 reshape.44
  1.6 4.8 %all-to-all-start = ((f32[8,1,1536]{2,1,0:T(1,128)}), f32[8,1,1536]{2,1,0:T(1,128)S(1)}, u32[]{:S(2)}, u32[]{:S(2)}) async-start(f32[8,1,1536]{2,1,0:T(1,128)} %reshape.44), calls=%async_computation | async-start | bytes 98304 | tf_op jit(solution)/shard_map/all_to_all | solution.py:68
  6.4 2.8 %fusion.21 = (f32[4,32,1,512]{3,2,1,0:T(1,128)S(1)}, f32[4,32,1,512]{3,2,1,0:T(1,128)S(1)}) fusion(f32[4,32,8,512]{3,2,1,0:T(8,128)} %param.6), kind=kLoop, calls=%fused_computation.53 | loop fusion | bytes 1048576 | tf_op jit(solution)/shard_map/slice | solution.py:30
  9.2 0.7 copy.16
  9.9 3.8 %collective-permute-start = (f32[4,32,1,512]{3,1,2,0:T(8,128)}, f32[4,32,1,512]{3,1,2,0:T(8,128)}, u32[]{:S(2)}, u32[]{:S(2)}) collective-permute-start(f32[4,32,1,512]{3,1,2,0:T(8,128)} %copy.16), channel_id=1, source_target_pairs={{0,8},{8,16},{16,24},{24,32},{32,40},{40,48},{48,56},{56,64},{64,7... | collective-permute-start | bytes 786440 | tf_op jit(solution)/shard_map/ppermute | solution.py:31
  13.7 0.7 copy.17
  14.4 9.7 %collective-permute-start.1 = (f32[4,32,1,512]{3,1,2,0:T(8,128)}, f32[4,32,1,512]{3,1,2,0:T(8,128)}, u32[]{:S(2)}, u32[]{:S(2)}) collective-permute-start(f32[4,32,1,512]{3,1,2,0:T(8,128)} %copy.17), channel_id=1, source_target_pairs={{8,0},{16,8},{24,16},{32,24},{40,32},{48,40},{56,48},{64,56},{72,6... | collective-permute-start | bytes 786440 | tf_op jit(solution)/shard_map/ppermute | solution.py:32
  24.3 1.9 %rsqrt_multiply_fusion = f32[4,32,8,511]{3,2,1,0:T(8,128)} fusion(f32[4,32,8,512]{3,2,1,0:T(8,128)S(1)} %copy-done), kind=kLoop, calls=%fused_computation.20 | loop fusion | flops 2093056 | bytes 6279168 | tf_op jit(solution)/shard_map/div | solution.py:38
  26.3 12.7 %all_gather.9 = f32[8,8,512]{2,1,0:T(8,128)S(1)} all-gather(f32[1,8,512]{2,1,0:T(8,128)S(1)} %slice.77), channel_id=1, replica_groups=mesh['rows'=64,'depth'=8] {'depth'}, dimensions={0}, use_global_device_ids=true | all-gather | bytes 147456 | tf_op jit(solution)/shard_map/all_gather | solution.py:12
  39.0 0.3 while.30
  39.3 0.2 fusion.9
  39.5 1.3 %copy-done.2 = f32[4,32,8,511]{3,2,1,0:T(8,128)S(1)} copy-done((f32[4,32,8,511]{3,2,1,0:T(8,128)S(1)}, f32[4,32,8,511]{3,2,1,0:T(8,128)}, u32[]{:S(2)}) %copy-start.2) | copy-done | bytes 2093080
  40.9 2.3 %maximum_multiply_fusion = f32[4,32,8,513]{3,2,1,0:T(8,128)} fusion(f32[4,32,8,1]{3,2,1,0:T(8,128)S(1)} %broadcast_in_dim.5, f32[4,32,8,511]{3,2,1,0:T(8,128)S(1)} %copy-done.2, f32[513]{0:T(1024)S(1)} %fusion.17), kind=kLoop, calls=%fused_computation.4 | loop fusion | flops 1575936 | bytes 4200452 | tf_op jit(solution)/shard_map/mul | solution.py:49
  43.1 0.5 broadcast.98
  43.6 0.8 reduce
  44.6 1.5 %multiply_reduce_fusion = (f32[32,8,512]{2,1,0:T(8,128)S(1)}, f32[3,32,8,512]{3,2,1,0:T(8,128)}) fusion(f32[4,32,8,512]{3,2,1,0:T(8,128)S(1)} %copy-done, f32[3,8,512]{2,1,0:T(8,128)S(1)} %mul.106, f32[32,8,512]{2,1,0:T(8,128)S(1)} %fusion.9), kind=kLoop, calls=%fused_computation.21 | loop fusion | flops 1048576 | bytes 4243456 | tf_op jit(solution)/shard_map/reduce_sum | solution.py:70
  46.1 0.8 %copy-done.4 = f32[32,8,512]{2,1,0:T(8,128)} copy-done((f32[32,8,512]{2,1,0:T(8,128)}, f32[32,8,512]{2,1,0:T(8,128)S(1)}, u32[]{:S(2)}) %copy-start.4) | copy-done | bytes 524312
  46.9 0.2 fusion.20
  47.1 12.7 %all-gather = f32[64,512]{1,0:T(8,128)S(1)} all-gather(f32[8,512]{1,0:T(8,128)S(1)} %fusion.19), channel_id=2, replica_groups=mesh['rows'=64,'depth'=8] {'depth'}, dimensions={0}, use_global_device_ids=true | all-gather | bytes 147456 | tf_op jit(solution)/shard_map/all_gather | solution.py:12
  59.9 0.3 while.31
  60.1 0.8 %rev.6 = f32[32,8,512]{2,1,0:T(8,128)} reverse(f32[32,8,512]{2,1,0:T(8,128)S(1)} %get-tuple-element.243), dimensions={0} | reverse | bytes 1048576 | tf_op jit(solution)/shard_map/rev | solution.py:79
  61.0 1.1 %fusion.22 = f32[32,8,512]{2,1,0:T(8,128)S(1)} fusion(f32[32,8,512]{2,1,0:T(8,128)} %rev.6), kind=kOutput, calls=%fused_computation.54 | output fusion | flops 4063232 | bytes 1048576 | tf_op jit(solution)/shard_map/jit(cumsum)/reduce_window_sum | solution.py:79
  62.1 1.4 %multiply_bitcast_fusion = f32[1,32,8,512]{3,2,1,0:T(8,128)S(1)} fusion(f32[32,8,512]{2,1,0:T(8,128)S(1)} %get-tuple-element.243, f32[32,8,512]{2,1,0:T(8,128)S(1)} %fusion.22, f32[32,8,512]{2,1,0:T(8,128)} %copy-done.4, f32[4,32,8,512]{3,2,1,0:T(8,128)S(1)} %copy-done, f32[8,512]{1,0:T(8,128)S(1)} %get-tuple-element.195, ...), kind=kLoop, calls=%fused_computation.36 | loop fusion | flops 1572864 | bytes 3178496 | tf_op jit(solution)/shard_map/broadcast_in_dim | solution.py:91
  63.5 1.2 %copy.12 = f32[4,32,1,512]{3,2,1,0:T(1,128)S(1)} copy(f32[4,32,1,512]{3,1,2,0:T(8,128)} %collective-permute-done) | data formatting | bytes 524288 | tf_op jit(solution)/shard_map/ppermute | solution.py:31
  64.7 1.2 %copy.13 = f32[4,32,1,512]{3,2,1,0:T(1,128)S(1)} copy(f32[4,32,1,512]{3,1,2,0:T(8,128)} %collective-permute-done.1) | data formatting | bytes 524288 | tf_op jit(solution)/shard_map/ppermute | solution.py:32
  66.0 2.8 %collective-permute-start.2 = (f32[4,1,10,512]{3,2,1,0:T(8,128)S(1)}, f32[4,1,10,512]{3,2,1,0:T(8,128)S(1)}, u32[]{:S(2)}, u32[]{:S(2)}) collective-permute-start(f32[4,1,10,512]{3,2,1,0:T(8,128)S(1)} %get-tuple-element.244), channel_id=1, source_target_pairs={{1,0},{2,1},{3,2},{4,3},{5,4},{6,5},{7,6},{9,8},{10,9},{11,10},{12... | collective-permute-start | bytes 245768 | tf_op jit(solution)/shard_map/ppermute | solution.py:32
  68.7 1.9 %collective-permute-start.3 = (f32[4,1,10,512]{3,2,1,0:T(8,128)S(1)}, f32[4,1,10,512]{3,2,1,0:T(8,128)S(1)}, u32[]{:S(2)}, u32[]{:S(2)}) collective-permute-start(f32[4,1,10,512]{3,2,1,0:T(8,128)S(1)} %get-tuple-element.245), channel_id=1, source_target_pairs={{0,1},{1,2},{2,3},{3,4},{4,5},{5,6},{6,7},{8,9},{9,10},{10,11},{11... | collective-permute-start | bytes 245768 | tf_op jit(solution)/shard_map/ppermute | solution.py:31
  70.7 1.4 %multiply_multiply_fusion = f32[4,32,9,512]{3,2,1,0:T(8,128)S(1)} fusion(f32[4,32,8,512]{3,2,1,0:T(8,128)S(1)} %copy-done, f32[4,32,1,512]{3,2,1,0:T(1,128)S(1)} %copy.12, f32[4,32,1,512]{3,2,1,0:T(1,128)S(1)} %copy.13, f32[9]{0:T(128)S(1)} %and_convert_fusion), kind=kLoop, calls=%fused_computation.3 | loop fusion | flops 4128768 | bytes 4980772 | tf_op jit(solution)/shard_map/mul | solution.py:49
  72.1 2.9 %collective-permute-done.3 = f32[4,1,10,512]{3,2,1,0:T(8,128)S(1)} collective-permute-done((f32[4,1,10,512]{3,2,1,0:T(8,128)S(1)}, f32[4,1,10,512]{3,2,1,0:T(8,128)S(1)}, u32[]{:S(2)}, u32[]{:S(2)}) %collective-permute-start.3) | collective-permute-done | bytes 81952 | tf_op jit(solution)/shard_map/ppermute | solution.py:31
  75.0 1.9 %multiply_multiply_fusion.1 = f32[4,33,8,512]{3,2,1,0:T(8,128)S(1)} fusion(f32[4,32,1,512]{3,2,1,0:T(1,128)S(1)} %copy.13, f32[4,32,8,512]{3,2,1,0:T(8,128)S(1)} %copy-done, f32[4,32,1,512]{3,2,1,0:T(1,128)S(1)} %copy.12, f32[4,1,10,512]{3,2,1,0:T(8,128)S(1)} %collective-permute-done.3, f32[4,1,10,512]{3,2,1,0:T(8,128)S(1)} %collective-permute-done.2, ...), kind=kLoop, calls=%fused_computation.12 | loop fusion | flops 5947392 | bytes 4948100 | tf_op jit(solution)/shard_map/mul | solution.py:49
  77.0 2.6 %fusion.3 = f32[4,32,8,512]{3,2,1,0:T(8,128)} fusion(f32[4,32,8,513]{3,2,1,0:T(8,128)S(1)} %copy-done.1, f32[4,32,9,512]{3,2,1,0:T(8,128)S(1)} %multiply_multiply_fusion, f32[4,33,8,512]{3,2,1,0:T(8,128)S(1)} %multiply_multiply_fusion.1, f32[3,32,8,512]{3,2,1,0:T(8,128)S(1)} %copy-done.3, f32[1,32,8,512]{3,2,1,0:T(8,128)S(1)} %multiply_bitcast_fusion), kind=kLoop, calls=%fused_computation.16 | loop fusion | flops 4194304 | bytes 16777216 | tf_op jit(solution)/shard_map/add | solution.py:103
  (42 shorter events, 0.7 us)
Async XLA Ops:
  0.0 24.1 %copy-start = (f32[4,32,8,512]{3,2,1,0:T(8,128)S(1)}, f32[4,32,8,512]{3,2,1,0:T(8,128)}, u32[]{:S(2)}) copy-start(f32[4,32,8,512]{3,2,1,0:T(8,128)} %param.6) | copy-start | bytes 6291460
  1.6 41.5 %all-to-all-start = ((f32[8,1,1536]{2,1,0:T(1,128)}), f32[8,1,1536]{2,1,0:T(1,128)S(1)}, u32[]{:S(2)}, u32[]{:S(2)}) async-start(f32[8,1,1536]{2,1,0:T(1,128)} %reshape.44), calls=%async_computation | async-start | bytes 98304 | tf_op jit(solution)/shard_map/all_to_all | solution.py:68
  9.9 53.5 %collective-permute-start = (f32[4,32,1,512]{3,1,2,0:T(8,128)}, f32[4,32,1,512]{3,1,2,0:T(8,128)}, u32[]{:S(2)}, u32[]{:S(2)}) collective-permute-start(f32[4,32,1,512]{3,1,2,0:T(8,128)} %copy.16), channel_id=1, source_target_pairs={{0,8},{8,16},{16,24},{24,32},{32,40},{40,48},{48,56},{56,64},{64,7... | collective-permute-start | bytes 786440 | tf_op jit(solution)/shard_map/ppermute | solution.py:31
  14.4 50.2 %collective-permute-start.1 = (f32[4,32,1,512]{3,1,2,0:T(8,128)}, f32[4,32,1,512]{3,1,2,0:T(8,128)}, u32[]{:S(2)}, u32[]{:S(2)}) collective-permute-start(f32[4,32,1,512]{3,1,2,0:T(8,128)} %copy.17), channel_id=1, source_target_pairs={{8,0},{16,8},{24,16},{32,24},{40,32},{48,40},{56,48},{64,56},{72,6... | collective-permute-start | bytes 786440 | tf_op jit(solution)/shard_map/ppermute | solution.py:32
  39.3 1.6 %copy-start.2 = (f32[4,32,8,511]{3,2,1,0:T(8,128)S(1)}, f32[4,32,8,511]{3,2,1,0:T(8,128)}, u32[]{:S(2)}) copy-start(f32[4,32,8,511]{3,2,1,0:T(8,128)} %rsqrt_multiply_fusion) | copy-start | bytes 6279172
  46.1 0.8 %copy-start.4 = (f32[32,8,512]{2,1,0:T(8,128)}, f32[32,8,512]{2,1,0:T(8,128)S(1)}, u32[]{:S(2)}) copy-start(f32[32,8,512]{2,1,0:T(8,128)S(1)} %get-tuple-element.248) | copy-start | bytes 1572868
  66.0 6.1 %collective-permute-start.2 = (f32[4,1,10,512]{3,2,1,0:T(8,128)S(1)}, f32[4,1,10,512]{3,2,1,0:T(8,128)S(1)}, u32[]{:S(2)}, u32[]{:S(2)}) collective-permute-start(f32[4,1,10,512]{3,2,1,0:T(8,128)S(1)} %get-tuple-element.244), channel_id=1, source_target_pairs={{1,0},{2,1},{3,2},{4,3},{5,4},{6,5},{7,6},{9,8},{10,9},{11,10},{12... | collective-permute-start | bytes 245768 | tf_op jit(solution)/shard_map/ppermute | solution.py:32
  68.7 6.3 %collective-permute-start.3 = (f32[4,1,10,512]{3,2,1,0:T(8,128)S(1)}, f32[4,1,10,512]{3,2,1,0:T(8,128)S(1)}, u32[]{:S(2)}, u32[]{:S(2)}) collective-permute-start(f32[4,1,10,512]{3,2,1,0:T(8,128)S(1)} %get-tuple-element.245), channel_id=1, source_target_pairs={{0,1},{1,2},{2,3},{3,4},{4,5},{5,6},{6,7},{8,9},{9,10},{10,11},{11... | collective-permute-start | bytes 245768 | tf_op jit(solution)/shard_map/ppermute | solution.py:31
  72.0 4.9 %copy-start.1 = (f32[4,32,8,513]{3,2,1,0:T(8,128)S(1)}, f32[4,32,8,513]{3,2,1,0:T(8,128)}, u32[]{:S(2)}) copy-start(f32[4,32,8,513]{3,2,1,0:T(8,128)} %maximum_multiply_fusion) | copy-start | bytes 6303748
  72.1 4.9 %copy-start.3 = (f32[3,32,8,512]{3,2,1,0:T(8,128)S(1)}, f32[3,32,8,512]{3,2,1,0:T(8,128)}, u32[]{:S(2)}) copy-start(f32[3,32,8,512]{3,2,1,0:T(8,128)} %get-tuple-element.249) | copy-start | bytes 4718596
